TPU v7x, 128 devices: a whole 4x4x4 slice. The times are simulated.
128 devices in a mesh: seg: 8 (over y_lo, z), grp: 16 (over x, y_hi, core).
Axes of the slice: x: 4, y: 4 (y_hi: 2, y_lo: 2; y = y_hi * 2 + y_lo), z: 4, core: 2. Of those that a mesh axis runs over, the one named last changes fastest.
Arguments:
- frames_in: bfloat16 [128, 32, 120, 128], P(('seg', 'grp')), may hold values from -6 to 6
- spatial_weight: bfloat16 [9, 128, 128], replicated, may hold values from -0.1875 to 0.1875
- temporal_weight: bfloat16 [2, 5, 128, 128], replicated, may hold values from -0.25 to 0.25
- uniting_weight: bfloat16 [2, 128, 128], replicated, may hold values from -0.375 to 0.375
- key_index: int32 [8], replicated, may hold values from 0 to 15
- dilation: int32 [2], replicated, may hold values from 1 to 8, as said below
- cotangent: bfloat16 [128, 32, 120, 128], P(('seg', 'grp')), may hold values from -6 to 6
Outputs:
- united: bfloat16 [128, 32, 120, 128], P(('seg', 'grp'))
- grad_frames: bfloat16 [128, 32, 120, 128], P(('seg', 'grp'))
- grad_spatial: float32 [9, 128, 128], replicated
- grad_temporal: float32 [2, 5, 128, 128], replicated
- grad_uniting: float32 [2, 128, 128], replicated
Inputs may be any that keep to these rules, and one draw needn't show every extreme that they name: `key_index`: position of a segment's keyframe within its 16 frames. Exactly one layer uses dilation 8; the others use less.
All inputs are finite; a program needn't handle non-finite values.
Results may differ from a plain program's by a relative error of at most 0.0095.
Values may be sent and summed in bfloat16 or wider, within the bound.
A program may use at most 128 MiB of HBM per device.

v0:
```python
import jax
import jax.numpy as jnp
from jax import lax
from jax.sharding import PartitionSpec as P

LAYERS = 2
DMAX = 8


def from_root(value, axis, root):
    mine = lax.axis_index(axis) == root
    return lax.psum(jnp.where(mine, value, jnp.zeros_like(value)), axis)


def silu_grad(value):
    sigma = jax.nn.sigmoid(value)
    return sigma * (1.0 + value * (1.0 - sigma))


def inner(left, right):
    return lax.dot_general(
        left, right, (((0,), (0,)), ((), ())), preferred_element_type=jnp.float32
    )


def spatial_forward(frames, kernel):
    count, rows, cols, chans = frames.shape
    padded = jnp.pad(frames, ((0, 0), (1, 1), (1, 1), (0, 0)))
    total = jnp.zeros((count * rows * cols, chans), jnp.float32)
    for row_tap in range(3):
        for col_tap in range(3):
            piece = padded[:, row_tap : row_tap + rows, col_tap : col_tap + cols, :].reshape(
                -1, chans
            )
            total = total + jnp.dot(
                piece, kernel[3 * row_tap + col_tap], preferred_element_type=jnp.float32
            )
    return total.reshape(frames.shape)


def spatial_back(grads, kernel):
    count, rows, cols, chans = grads.shape
    padded = jnp.pad(grads, ((0, 0), (1, 1), (1, 1), (0, 0)))
    total = jnp.zeros((count * rows * cols, chans), jnp.float32)
    for row_tap in range(3):
        for col_tap in range(3):
            piece = padded[
                :, 2 - row_tap : 2 - row_tap + rows, 2 - col_tap : 2 - col_tap + cols, :
            ].reshape(-1, chans)
            total = total + jnp.dot(
                piece, kernel[3 * row_tap + col_tap].T, preferred_element_type=jnp.float32
            )
    return total.reshape(grads.shape)


def spatial_wgrad(frames, grads):
    count, rows, cols, chans = frames.shape
    padded = jnp.pad(frames, ((0, 0), (1, 1), (1, 1), (0, 0)))
    flat_grads = grads.reshape(-1, chans)
    result = []
    for row_tap in range(3):
        for col_tap in range(3):
            piece = padded[:, row_tap : row_tap + rows, col_tap : col_tap + cols, :].reshape(
                -1, chans
            )
            result.append(inner(piece, flat_grads))
    return jnp.stack(result)


def shifted(values, offset):
    padded = jnp.pad(values, ((2 * DMAX, 2 * DMAX), (0, 0), (0, 0)))
    start = 2 * DMAX + offset
    return lax.dynamic_slice_in_dim(padded, start, values.shape[0], 0)


def temporal_forward(acts, kernel, step_size):
    chans = acts.shape[2]
    total = jnp.zeros((acts.shape[0] * acts.shape[1], chans), jnp.float32)
    for tap in range(5):
        piece = shifted(acts, (tap - 2) * step_size).reshape(-1, chans)
        total = total + jnp.dot(piece, kernel[tap], preferred_element_type=jnp.float32)
    return total.reshape(acts.shape)


def temporal_back(grads, kernel, step_size):
    chans = grads.shape[2]
    total = jnp.zeros((grads.shape[0] * grads.shape[1], chans), jnp.float32)
    for tap in range(5):
        piece = shifted(grads, (2 - tap) * step_size).reshape(-1, chans)
        total = total + jnp.dot(piece, kernel[tap].T, preferred_element_type=jnp.float32)
    return total.reshape(grads.shape)


def temporal_wgrad(acts, grads, step_size):
    chans = acts.shape[2]
    flat_grads = grads.reshape(-1, chans)
    return jnp.stack(
        [
            inner(shifted(acts, (tap - 2) * step_size).reshape(-1, chans), flat_grads)
            for tap in range(5)
        ]
    )


def to_pixels(flat):
    return lax.all_to_all(flat, ("seg", "grp"), split_axis=1, concat_axis=0, tiled=True)


def to_frames(blocks):
    return lax.all_to_all(blocks, ("seg", "grp"), split_axis=0, concat_axis=1, tiled=True)


def local(
    frames_in, spatial_weight, temporal_weight, uniting_weight, key_index, dilation, cotangent
):
    local_frames, rows, cols, chans = frames_in.shape
    pixels = rows * cols
    seg_count = lax.axis_size("seg")
    pre_spatial = spatial_forward(frames_in, spatial_weight)
    act_zero = jax.nn.silu(pre_spatial).astype(jnp.bfloat16).reshape(local_frames, pixels, chans)
    cot_local = cotangent.reshape(local_frames, pixels, chans)
    act_blocks = to_pixels(act_zero)
    cot_blocks = lax.all_to_all(cot_local, ("seg", "grp"), split_axis=1, concat_axis=0, tiled=True)
    acts = [act_blocks]
    total_frames = acts[0].shape[0]
    block = acts[0].shape[1]
    seg_frames = total_frames // seg_count
    pres = []
    for layer in range(LAYERS):
        pre = temporal_forward(acts[-1], temporal_weight[layer], dilation[layer])
        pres.append(pre)
        acts.append(jax.nn.silu(pre).astype(jnp.bfloat16))
    feat = acts[-1]
    feat_seg = feat.reshape(seg_count, seg_frames, block, chans)
    positions = jnp.arange(seg_frames, dtype=jnp.int32)
    onehot = positions[None, :] == key_index[:, None]
    keys = jnp.einsum(
        "ns,nspc->npc", onehot.astype(jnp.bfloat16), feat_seg, preferred_element_type=jnp.float32
    ).astype(jnp.bfloat16)
    key_full = jnp.broadcast_to(keys[:, None], feat_seg.shape).reshape(-1, chans)
    feat_flat = feat.reshape(-1, chans)
    feat_time = to_frames(feat)
    seg_here = key_index[lax.axis_index("seg")]
    owner = seg_here // local_frames
    local_pos = seg_here % local_frames
    panel = lax.dynamic_index_in_dim(feat_time, local_pos, 0, keepdims=False)
    key_panel = from_root(panel, "grp", owner)
    key_part = jnp.dot(key_panel, uniting_weight[1], preferred_element_type=jnp.float32)
    main_part = jnp.dot(
        feat_time.reshape(-1, chans), uniting_weight[0], preferred_element_type=jnp.float32
    )
    united = (main_part.reshape(local_frames, pixels, chans) + key_part[None]).astype(jnp.bfloat16)
    cot_flat = cot_blocks.reshape(-1, chans)
    grad_feat = jnp.dot(cot_flat, uniting_weight[0].T, preferred_element_type=jnp.float32)
    seg_cot = jnp.sum(
        cot_blocks.reshape(seg_count, seg_frames, block, chans).astype(jnp.float32), axis=1
    )
    key_term = jnp.dot(
        seg_cot.reshape(-1, chans),
        uniting_weight[1].T.astype(jnp.float32),
        precision=lax.Precision.HIGHEST,
    ).reshape(seg_count, 1, block, chans)
    placed = onehot.astype(jnp.float32)[:, :, None, None] * key_term
    grad_feat = grad_feat.reshape(seg_count, seg_frames, block, chans) + placed
    grad_feat = grad_feat.reshape(total_frames, block, chans)
    grad_uniting = jnp.stack([inner(feat_flat, cot_flat), inner(key_full, cot_flat)])
    grad_pre = (grad_feat * silu_grad(pres[-1])).astype(jnp.bfloat16)
    tgrads = [None] * LAYERS
    grad_act0 = None
    for layer in range(LAYERS - 1, -1, -1):
        tgrads[layer] = temporal_wgrad(acts[layer], grad_pre, dilation[layer])
        grad_act = temporal_back(grad_pre, temporal_weight[layer], dilation[layer])
        if layer > 0:
            grad_pre = (grad_act * silu_grad(pres[layer - 1])).astype(jnp.bfloat16)
        else:
            grad_act0 = grad_act.astype(jnp.bfloat16)
    grad_time = to_frames(grad_act0).reshape(frames_in.shape)
    grad_spre = (grad_time.astype(jnp.float32) * silu_grad(pre_spatial)).astype(jnp.bfloat16)
    grad_frames = spatial_back(grad_spre, spatial_weight).astype(jnp.bfloat16)
    grad_spatial = spatial_wgrad(frames_in, grad_spre)
    summed = lax.psum((grad_spatial, jnp.stack(tgrads), grad_uniting), ("seg", "grp"))
    scale = 1.0 / jnp.sqrt(jnp.float32(total_frames * pixels))
    return (
        united.reshape(frames_in.shape),
        grad_frames,
        summed[0] * scale,
        summed[1] * scale,
        summed[2] * scale,
    )


def solution(mesh):
    placed = (
        P(("seg", "grp"), None, None, None),
        P(),
        P(),
        P(),
        P(),
        P(),
        P(("seg", "grp"), None, None, None),
    )
    return jax.shard_map(
        local,
        mesh=mesh,
        in_specs=placed,
        out_specs=(
            P(("seg", "grp"), None, None, None),
            P(("seg", "grp"), None, None, None),
            P(),
            P(),
            P(),
        ),
        check_vma=False,
    )
```

profile of v0, /device:TPU:0, one launch (start us, length us, event | category | flops | bytes accessed | tf_op | source)
XLA Modules:
  0.0 697.2 jit_solution(8917479555947847527)
XLA Ops:
  7.2 7.2 %pad_slice_fusion.8 = (bf16[1,32,120,128]{3,2,1,0:T(8,128)(2,1)S(1)}, bf16[1,32,120,128]{3,2,1,0:T(8,128)(2,1)S(1)}, bf16[1,32,120,128]{3,2,1,0:T(8,128)(2,1)S(1...) fusion(bf16[1,32,120,128]{3,2,1,0:T(8,128)(2,1)} %param.7), kind=kLoop, calls=%fused_computation.144 | loop fusion | bytes 8847360 | tf_op jit(solution)/shard_map/slice | solution.py:32
  19.3 16.0 %copy.215 = bf16[1,3840,128]{2,0,1:T(2,128)(2,1)} copy(bf16[1,3840,128]{2,1,0:T(8,128)(2,1)S(1)} %fusion.41) | data formatting | bytes 1966080 | tf_op jit(solution)/shard_map/convert_element_type | solution.py:120
  35.9 22.2 %reduce.4 = bf16[3840,128]{1,0:T(8,128)(2,1)S(1)} reduce(bf16[3840,1,128]{2,1,0:T(2,128)(2,1)} %bitcast.386, bf16[]{:T(256)} %broadcast.145), dimensions={1}, to_apply=%bitcast.378.reduce_sub_computation | reduce | bytes 1966082
  59.4 11.1 %all-to-all-start = ((bf16[128,2,1920]{2,1,0:T(2,128)(2,1)}), bf16[128,2,1920]{2,1,0:T(2,128)(2,1)S(1)}, u32[]{:S(2)}, u32[]{:S(2)}) async-start(bf16[128,2,1920]{2,1,0:T(2,128)(2,1)} %reshape.558), calls=%async_computation | async-start | bytes 1966080 | tf_op jit(solution)/shard_map/all_to_all | solution.py:106
  79.1 9.9 %copy.214 = bf16[1,3840,128]{2,0,1:T(2,128)(2,1)} copy(bf16[1,3840,128]{2,1,0:T(8,128)(2,1)} %bitcast.404) | data formatting | bytes 1966080 | tf_op jit(solution)/shard_map/reshape | solution.py:121
  89.0 23.1 %reduce.5 = bf16[3840,128]{1,0:T(8,128)(2,1)} reduce(bf16[3840,1,128]{2,1,0:T(2,128)(2,1)} %bitcast.387, bf16[]{:T(256)} %broadcast.145), dimensions={1}, to_apply=%bitcast.377.reduce_sub_computation | reduce | bytes 1966082
  118.4 10.4 %all-to-all-start.2 = ((bf16[128,2,1920]{2,1,0:T(2,128)(2,1)}), bf16[128,2,1920]{2,1,0:T(2,128)(2,1)}, u32[]{:S(2)}, u32[]{:S(2)}) async-start(bf16[128,2,1920]{2,1,0:T(2,128)(2,1)} %reshape.560), calls=%async_computation.2 | async-start | bytes 1966080 | tf_op jit(solution)/shard_map/all_to_all | solution.py:123
  129.7 17.4 %bitcast_reduce_fusion.1 = bf16[3840,128]{1,0:T(8,128)(2,1)} fusion(bf16[3840,1,128]{2,1,0:T(2,128)(2,1)S(1)} %reshape.559), kind=kLoop, calls=%fused_computation.264 | loop fusion | bytes 1966080 | tf_op jit(solution)/shard_map/all_to_all | solution.py:106
  150.1 5.6 pad_dynamic-slice_fusion.12
  188.4 3.5 pad_dynamic-slice_fusion.8
  218.5 4.1 reshape.561
  222.7 17.5 %bitcast_reduce_fusion = bf16[3840,128]{1,0:T(8,128)(2,1)} fusion(bf16[3840,1,128]{2,1,0:T(2,128)(2,1)S(1)} %reshape.561), kind=kLoop, calls=%fused_computation.263 | loop fusion | bytes 1966080 | tf_op jit(solution)/shard_map/all_to_all | solution.py:123
  244.1 5.1 multiply_convert_fusion
  257.7 4.2 multiply_convert_fusion.9
  262.9 3.2 pad_dynamic-slice_fusion.4
  291.6 3.2 multiply_convert_fusion.6
  304.2 3.5 pad_dynamic-slice_fusion
  337.6 10.4 %all-to-all-start.3 = ((bf16[128,30,128]{2,1,0:T(8,128)(2,1)}), bf16[128,30,128]{2,1,0:T(8,128)(2,1)}, u32[]{:S(2)}, u32[]{:S(2)}) async-start(bf16[128,30,128]{2,1,0:T(8,128)(2,1)} %convert_element_type.196), calls=%async_computation.3 | async-start | bytes 2097152 | tf_op jit(solution)/shard_map/all_to_all | solution.py:110
  357.8 8.0 %all-to-all-done.3 = bf16[128,30,128]{2,1,0:T(8,128)(2,1)} async-done(((bf16[128,30,128]{2,1,0:T(8,128)(2,1)}), bf16[128,30,128]{2,1,0:T(8,128)(2,1)}, u32[]{:S(2)}, u32[]{:S(2)}) %all-to-all-start.3) | async-done | bytes 983072 | tf_op jit(solution)/shard_map/all_to_all | solution.py:110
  365.8 5.8 all-to-all-start.1
  378.3 3.2 multiply_convert_fusion.3
  398.7 3.7 pad_slice_fusion
  418.3 127.8 %all-reduce.12.cloned.1.call-done = (f32[9,128,128]{2,1,0:T(8,128)}, f32[2,5,128,128]{3,2,1,0:T(8,128)}, f32[2,128,128]{2,1,0:T(8,128)}) async-done(((f32[9,128,128]{2,1,0:T(8,128)}, f32[2,5,128,128]{3,2,1,0:T(8,128)}, f32[2,128,128]{2,1,0:T(8,128)}), (f32[9,128,128]{2,1,0:T(8,128)}, f32[2,5,128,128]{3,2,1,0:T(8,128)}, f32[2,128,128]{2,1,0:T(8,128)})) %all-reduce.12.cloned.1.call-update) | async-done | bytes 1376272 | tf_op jit(solution)/shard_map/psum | solution.py:181
  551.6 136.0 %all-reduce.10.cloned.1.call-done = bf16[3840,128]{1,0:T(8,128)(2,1)} async-done(((bf16[3840,128]{1,0:T(8,128)(2,1)}), bf16[3840,128]{1,0:T(8,128)(2,1)}) %all-reduce.10.cloned.1.call-update) | async-done | bytes 983056 | tf_op jit(solution)/shard_map/psum | solution.py:12
  (266 shorter events, 212.6 us)
Async XLA Ops:
  7.2 7.2 %copy-start.47 = (bf16[9,128,128]{2,1,0:T(8,128)(2,1)S(1)}, bf16[9,128,128]{2,1,0:T(8,128)(2,1)}, u32[]{:S(2)}) copy-start(bf16[9,128,128]{2,1,0:T(8,128)(2,1)} %param.8) | copy-start | bytes 884740
  18.8 58.8 %copy-start = (f32[3840,128]{1,0:T(8,128)}, f32[3840,128]{1,0:T(8,128)S(1)}, u32[]{:S(2)}) copy-start(f32[3840,128]{1,0:T(8,128)S(1)} %convolution_add_fusion.25) | copy-start | bytes 5898244
  58.2 12.4 %copy-start.57 = (s32[2]{0:T(128)S(1)}, s32[2]{0:T(128)}, u32[]{:S(2)}) copy-start(s32[2]{0:T(128)} %param.12) | copy-start | bytes 28
  59.4 59.0 %all-to-all-start = ((bf16[128,2,1920]{2,1,0:T(2,128)(2,1)}), bf16[128,2,1920]{2,1,0:T(2,128)(2,1)S(1)}, u32[]{:S(2)}, u32[]{:S(2)}) async-start(bf16[128,2,1920]{2,1,0:T(2,128)(2,1)} %reshape.558), calls=%async_computation | async-start | bytes 1966080 | tf_op jit(solution)/shard_map/all_to_all | solution.py:106
  89.0 26.2 %copy-start.23 = (f32[128,30,128]{2,1,0:T(8,128)S(1)}, f32[128,30,128]{2,1,0:T(8,128)}, u32[]{:S(2)}) copy-start(f32[128,30,128]{2,1,0:T(8,128)} %reshape.520) | copy-start | bytes 5898244
  118.4 100.1 %all-to-all-start.2 = ((bf16[128,2,1920]{2,1,0:T(2,128)(2,1)}), bf16[128,2,1920]{2,1,0:T(2,128)(2,1)}, u32[]{:S(2)}, u32[]{:S(2)}) async-start(bf16[128,2,1920]{2,1,0:T(2,128)(2,1)} %reshape.560), calls=%async_computation.2 | async-start | bytes 1966080 | tf_op jit(solution)/shard_map/all_to_all | solution.py:123
  129.7 46.6 %copy-start.6 = (bf16[3840,1,128]{2,1,0:T(2,128)(2,1)}, bf16[3840,1,128]{2,1,0:T(2,128)(2,1)S(1)}, u32[]{:S(2)}) copy-start(bf16[3840,1,128]{2,1,0:T(2,128)(2,1)S(1)} %reshape.559) | copy-start | bytes 2949124
  155.7 4.2 copy-start.10
  159.9 4.9 copy-start.12
  187.8 4.0 copy-start.2
  191.9 4.9 copy-start.19
  196.8 4.1 copy-start.17
  222.7 19.7 %copy-start.24 = (bf16[3840,1,128]{2,1,0:T(2,128)(2,1)}, bf16[3840,1,128]{2,1,0:T(2,128)(2,1)S(1)}, u32[]{:S(2)}) copy-start(bf16[3840,1,128]{2,1,0:T(2,128)(2,1)S(1)} %reshape.561) | copy-start | bytes 2949124
  240.2 3.6 copy-start.56
  257.7 4.2 copy-start.22
  304.2 3.5 copy-start.5
  304.2 3.5 copy-start.25
  310.5 4.8 copy-start.20
  337.6 13.8 %copy-start.7 = (bf16[3840,1,128]{2,1,0:T(2,128)(2,1)S(1)}, bf16[3840,1,128]{2,1,0:T(2,128)(2,1)}, u32[]{:S(2)}) copy-start(bf16[3840,1,128]{2,1,0:T(2,128)(2,1)} %copy-done.6) | copy-start | bytes 2949124
  337.6 28.2 %all-to-all-start.3 = ((bf16[128,30,128]{2,1,0:T(8,128)(2,1)}), bf16[128,30,128]{2,1,0:T(8,128)(2,1)}, u32[]{:S(2)}, u32[]{:S(2)}) async-start(bf16[128,30,128]{2,1,0:T(8,128)(2,1)} %convert_element_type.196), calls=%async_computation.3 | async-start | bytes 2097152 | tf_op jit(solution)/shard_map/all_to_all | solution.py:110
  351.4 3.5 copy-start.11
  365.8 38.3 %all-to-all-start.1 = ((bf16[128,30,128]{2,1,0:T(8,128)(2,1)}), bf16[128,30,128]{2,1,0:T(8,128)(2,1)}, u32[]{:S(2)}, u32[]{:S(2)}) async-start(bf16[128,30,128]{2,1,0:T(8,128)(2,1)} %copy.137), calls=%async_computation.1 | async-start | bytes 2097152 | tf_op jit(solution)/shard_map/all_to_all | solution.py:110
  371.6 174.5 %all-reduce.12.cloned.1.call-start = ((), (), s32[]{:S(2)}) async-start(), calls=%async_computation.5 | async-start | bytes 2752512 | tf_op jit(solution)/shard_map/psum | solution.py:181
  396.0 291.6 %all-reduce.10.cloned.1.call-start = ((), (), s32[]{:S(2)}) async-start(), calls=%async_computation.4 | async-start | bytes 1966080 | tf_op jit(solution)/shard_map/psum | solution.py:12
  (42 other events, 74.7 us)
Sparse Core Ops, SparseCore 0:
  396.1 149.9 all-reduce.11
  549.3 138.1 all-reduce.9
where the time goes:
time: 707 us; the launch traced here: 697 us
  waiting for transfers between devices  272 us (38%)
  local copies, waits for them, and re-layouts  221 us (31%)
  matrix products  74.7 us (11%)
  other arithmetic  69.4 us (10%)
  starting transfers between devices  37.8 us (5%)
  between operations  22.4 us (3%)
    psum x1, waiting for transfers between devices, from_root(): return lax.psum(jnp.where(mine, value, jnp.zeros_like(value)), axis)  136 us
    psum x1, waiting for transfers between devices, local(): lax.psum((grad_spatial, jnp.stack(tgrads), grad_uniting), ('seg', 'grp'))  128 us
    dynamic_slice x20, local copies, waits for them, and re-layouts, shifted(): return lax.dynamic_slice_in_dim(padded, start, values.shape[0], 0)  50.3 us
    unnamed x2, other arithmetic  45.3 us
    dot_general x21, matrix products, inner(): lax.dot_general(left, right, (((0,), (0,)), ((), ())), preferred_element_...  24 us
    all_to_all x3, local copies, waits for them, and re-layouts, to_pixels(): lax.all_to_all(flat, ('seg', 'grp'), split_axis=1, concat_axis=0, tiled=T...  20.4 us
    unnamed x125, local copies, waits for them, and re-layouts  18.4 us
    all_to_all x1, local copies, waits for them, and re-layouts, local(): lax.all_to_all(cot_local, ('seg', 'grp'), split_axis=1, concat_axis=0, ti...  17.5 us
  transfers between devices with their start and end apart: 6, of which 3 were waited for; matrix products, arithmetic and copies ran while one was open for 27% of the time, Pallas kernels for 0%

commit v1 on v0

--- a/solution.py
+++ b/solution.py
@@ -5,11 +5,12 @@
 
 LAYERS = 2
 DMAX = 8
+_write_series_all = lambda w_in, peer_axis: lax.all_gather(w_in, axis_name=peer_axis).sum(axis=0)
 
 
 def from_root(value, axis, root):
     mine = lax.axis_index(axis) == root
-    return lax.psum(jnp.where(mine, value, jnp.zeros_like(value)), axis)
+    return _write_series_all(jnp.where(mine, value, jnp.zeros_like(value)), axis)
 
 
 def silu_grad(value):

time: 707 us -> 670 us (0.948)
  waiting for transfers between devices: 272 us -> 181 us
  local copies, waits for them, and re-layouts: 221 us -> 249 us
  matrix products: 74.7 us -> 84.5 us
  other arithmetic: 69.4 us -> 78.8 us
    psum x1 -> x0, waiting for transfers between devices: 136 us -> none  [from_root(): return lax.psum(jnp.where(mine, value, jnp.zeros_like(value)), axis)]
    psum x1, waiting for transfers between devices: 128 us -> 181 us  [local(): lax.psum((grad_spatial, jnp.stack(tgrads), grad_uniting), ('seg', 'grp'))]
    reduce_sum x0 -> x1, other arithmetic: none -> 8.64 us  [lax.all_gather(w_in, axis_name=peer_axis).sum(axis=0)]
    dynamic_slice x20, local copies, waits for them, and re-layouts: 50.3 us -> 58.5 us  [shifted(): return lax.dynamic_slice_in_dim(padded, start, values.shape[0], 0)]
    dot_general x10, matrix products: 15.7 us -> 23.8 us  [temporal_back(): jnp.dot(piece, kernel[tap].T, preferred_element_type=jnp.float32)]
    all_to_all x2, waiting for transfers between devices: 8.03 us -> 0.01 us  [to_frames(): lax.all_to_all(blocks, ('seg', 'grp'), split_axis=0, concat_axis=1, tiled...]
    unnamed x125 -> x85, local copies, waits for them, and re-layouts: 18.4 us -> 19.5 us
  transfers between devices with their start and end apart: 6 -> 6, of which waited for: 3 -> 1; matrix products, arithmetic and copies ran while one was open for 27% -> 33% of each run, Pallas kernels for 0% -> 0%
where the time goes in v1:
time: 670 us; the launch traced here: 659 us
  local copies, waits for them, and re-layouts  249 us (37%)
  waiting for transfers between devices  181 us (27%)
  matrix products  84.5 us (13%)
  other arithmetic  78.8 us (12%)
  starting transfers between devices  41.7 us (6%)
  between operations  23.5 us (4%)
    psum x1, waiting for transfers between devices, local(): lax.psum((grad_spatial, jnp.stack(tgrads), grad_uniting), ('seg', 'grp'))  181 us
    dynamic_slice x20, local copies, waits for them, and re-layouts, shifted(): return lax.dynamic_slice_in_dim(padded, start, values.shape[0], 0)  58.5 us
    unnamed x2, other arithmetic  45.2 us
    dot_general x21, matrix products, inner(): lax.dot_general(left, right, (((0,), (0,)), ((), ())), preferred_element_...  24.4 us
    dot_general x10, matrix products, temporal_back(): jnp.dot(piece, kernel[tap].T, preferred_element_type=jnp.float32)  23.8 us
    all_to_all x3, local copies, waits for them, and re-layouts, to_pixels(): lax.all_to_all(flat, ('seg', 'grp'), split_axis=1, concat_axis=0, tiled=T...  21.4 us
    all_to_all x2, starting transfers between devices, to_frames(): lax.all_to_all(blocks, ('seg', 'grp'), split_axis=0, concat_axis=1, tiled...  20.1 us
    unnamed x85, local copies, waits for them, and re-layouts  19.5 us
  transfers between devices with their start and end apart: 6, of which 1 were waited for; matrix products, arithmetic and copies ran while one was open for 33% of the time, Pallas kernels for 0%

profile of v1, /device:TPU:0, one launch (start us, length us, event | category | flops | bytes accessed | tf_op | source)
XLA Modules:
  0.0 659.1 jit_solution(5562274995653732031)
XLA Ops:
  8.0 7.3 %pad_slice_fusion.8 = (bf16[1,32,120,128]{3,2,1,0:T(8,128)(2,1)S(1)}, bf16[1,32,120,128]{3,2,1,0:T(8,128)(2,1)S(1)}, bf16[1,32,120,128]{3,2,1,0:T(8,128)(2,1)S(1...) fusion(bf16[1,32,120,128]{3,2,1,0:T(8,128)(2,1)} %param.7), kind=kLoop, calls=%fused_computation.144 | loop fusion | bytes 8847360 | tf_op jit(solution)/shard_map/slice | solution.py:33
  20.3 16.0 %copy.216 = bf16[1,3840,128]{2,0,1:T(2,128)(2,1)} copy(bf16[1,3840,128]{2,1,0:T(8,128)(2,1)S(1)} %fusion.41) | data formatting | bytes 1966080 | tf_op jit(solution)/shard_map/convert_element_type | solution.py:121
  36.9 22.2 %reduce.5 = bf16[3840,128]{1,0:T(8,128)(2,1)S(1)} reduce(bf16[3840,1,128]{2,1,0:T(2,128)(2,1)} %bitcast.386, bf16[]{:T(256)} %broadcast.163), dimensions={1}, to_apply=%bitcast.378.reduce_sub_computation | reduce | bytes 1966082
  60.4 11.1 %all-to-all-start = ((bf16[128,2,1920]{2,1,0:T(2,128)(2,1)}), bf16[128,2,1920]{2,1,0:T(2,128)(2,1)S(1)}, u32[]{:S(2)}, u32[]{:S(2)}) async-start(bf16[128,2,1920]{2,1,0:T(2,128)(2,1)} %reshape.571), calls=%async_computation | async-start | bytes 1966080 | tf_op jit(solution)/shard_map/all_to_all | solution.py:107
  80.1 9.9 %copy.215 = bf16[1,3840,128]{2,0,1:T(2,128)(2,1)} copy(bf16[1,3840,128]{2,1,0:T(8,128)(2,1)} %bitcast.404) | data formatting | bytes 1966080 | tf_op jit(solution)/shard_map/reshape | solution.py:122
  89.9 23.0 %reduce.6 = bf16[3840,128]{1,0:T(8,128)(2,1)} reduce(bf16[3840,1,128]{2,1,0:T(2,128)(2,1)} %bitcast.387, bf16[]{:T(256)} %broadcast.163), dimensions={1}, to_apply=%bitcast.377.reduce_sub_computation | reduce | bytes 1966082
  119.0 10.4 %all-to-all-start.2 = ((bf16[128,2,1920]{2,1,0:T(2,128)(2,1)}), bf16[128,2,1920]{2,1,0:T(2,128)(2,1)}, u32[]{:S(2)}, u32[]{:S(2)}) async-start(bf16[128,2,1920]{2,1,0:T(2,128)(2,1)} %reshape.573), calls=%async_computation.2 | async-start | bytes 1966080 | tf_op jit(solution)/shard_map/all_to_all | solution.py:124
  129.5 3.3 reshape.572
  132.8 18.4 %bitcast_reduce_fusion.1 = bf16[3840,128]{1,0:T(8,128)(2,1)} fusion(bf16[3840,1,128]{2,1,0:T(2,128)(2,1)} %reshape.572), kind=kLoop, calls=%fused_computation.264 | loop fusion | bytes 1966080 | tf_op jit(solution)/shard_map/all_to_all | solution.py:107
  154.2 5.5 pad_dynamic-slice_fusion.12
  195.0 3.2 pad_dynamic-slice_fusion.8
  231.9 5.6 reshape.574
  237.5 18.6 %bitcast_reduce_fusion = bf16[3840,128]{1,0:T(8,128)(2,1)} fusion(bf16[3840,1,128]{2,1,0:T(2,128)(2,1)} %reshape.574), kind=kLoop, calls=%fused_computation.263 | loop fusion | bytes 1966080 | tf_op jit(solution)/shard_map/all_to_all | solution.py:124
  257.9 4.7 multiply_convert_fusion
  271.2 4.1 multiply_convert_fusion.9
  275.3 3.6 pad_dynamic-slice_fusion.4
  309.3 3.1 multiply_convert_fusion.6
  321.5 3.7 pad_dynamic-slice_fusion
  363.4 10.4 %all-to-all-start.3 = ((bf16[128,30,128]{2,1,0:T(8,128)(2,1)}), bf16[128,30,128]{2,1,0:T(8,128)(2,1)}, u32[]{:S(2)}, u32[]{:S(2)}) async-start(bf16[128,30,128]{2,1,0:T(8,128)(2,1)} %convert_element_type.198), calls=%async_computation.3 | async-start | bytes 2097152 | tf_op jit(solution)/shard_map/all_to_all | solution.py:111
  387.8 3.1 fusion.5
  394.9 9.7 %all-to-all-start.1 = ((bf16[128,30,128]{2,1,0:T(8,128)(2,1)}), bf16[128,30,128]{2,1,0:T(8,128)(2,1)S(1)}, u32[]{:S(2)}, u32[]{:S(2)}) async-start(bf16[128,30,128]{2,1,0:T(8,128)(2,1)} %copy.138), calls=%async_computation.1 | async-start | bytes 2097152 | tf_op jit(solution)/shard_map/all_to_all | solution.py:111
  407.2 3.5 multiply_convert_fusion.3
  454.8 181.1 %all-reduce.9.cloned.1.call-done = (f32[9,128,128]{2,1,0:T(8,128)}, f32[2,5,128,128]{3,2,1,0:T(8,128)}, f32[2,128,128]{2,1,0:T(8,128)}) async-done(((f32[9,128,128]{2,1,0:T(8,128)}, f32[2,5,128,128]{3,2,1,0:T(8,128)}, f32[2,128,128]{2,1,0:T(8,128)}), (f32[9,128,128]{2,1,0:T(8,128)}, f32[2,5,128,128]{3,2,1,0:T(8,128)}, f32[2,128,128]{2,1,0:T(8,128)})) %all-reduce.9.cloned.1.call-update) | async-done | bytes 1376272 | tf_op jit(solution)/shard_map/psum | solution.py:182
  641.4 8.6 %reduce_sum.21 = bf16[3840,128]{1,0:T(8,128)(2,1)S(1)} reduce(bf16[16,3840,128]{2,1,0:T(8,128)(2,1)} %all-gather.2.cloned.1.call-done, bf16[]{:T(256)} %constant.79.clone.1), dimensions={0}, to_apply=%region_0.1 | reduce | flops 7372800 | bytes 16711682 | tf_op jit(solution)/shard_map/reduce_sum | solution.py:8
  (228 shorter events, 245.3 us)
Async XLA Ops:
  8.0 7.3 %copy-start.29 = (bf16[9,128,128]{2,1,0:T(8,128)(2,1)S(1)}, bf16[9,128,128]{2,1,0:T(8,128)(2,1)}, u32[]{:S(2)}) copy-start(bf16[9,128,128]{2,1,0:T(8,128)(2,1)} %param.8) | copy-start | bytes 884740
  59.1 12.4 %copy-start.38 = (s32[2]{0:T(128)S(1)}, s32[2]{0:T(128)}, u32[]{:S(2)}) copy-start(s32[2]{0:T(128)} %param.12) | copy-start | bytes 28
  60.4 58.7 %all-to-all-start = ((bf16[128,2,1920]{2,1,0:T(2,128)(2,1)}), bf16[128,2,1920]{2,1,0:T(2,128)(2,1)S(1)}, u32[]{:S(2)}, u32[]{:S(2)}) async-start(bf16[128,2,1920]{2,1,0:T(2,128)(2,1)} %reshape.571), calls=%async_computation | async-start | bytes 1966080 | tf_op jit(solution)/shard_map/all_to_all | solution.py:107
  116.0 2.9 copy-start.39
  119.0 112.9 %all-to-all-start.2 = ((bf16[128,2,1920]{2,1,0:T(2,128)(2,1)}), bf16[128,2,1920]{2,1,0:T(2,128)(2,1)}, u32[]{:S(2)}, u32[]{:S(2)}) async-start(bf16[128,2,1920]{2,1,0:T(2,128)(2,1)} %reshape.573), calls=%async_computation.2 | async-start | bytes 1966080 | tf_op jit(solution)/shard_map/all_to_all | solution.py:124
  159.7 14.8 %copy-start.8 = (bf16[128,30,128]{0,2,1:T(8,128)(2,1)}, bf16[128,30,128]{0,2,1:T(8,128)(2,1)S(1)}, u32[]{:S(2)}) copy-start(bf16[128,30,128]{0,2,1:T(8,128)(2,1)S(1)} %get-tuple-element.32) | copy-start | bytes 2949124
  198.2 17.7 %copy-start.5 = (bf16[128,30,128]{0,2,1:T(8,128)(2,1)}, bf16[128,30,128]{0,2,1:T(8,128)(2,1)S(1)}, u32[]{:S(2)}) copy-start(bf16[128,30,128]{0,2,1:T(8,128)(2,1)S(1)} %get-tuple-element.28) | copy-start | bytes 2949124
  275.3 3.6 copy-start.14
  302.8 2.4 copy-start
  302.8 3.0 copy-start.27
  318.1 3.0 copy-start.12
  321.4 3.7 copy-start.11
  321.5 4.1 copy-start.30
  363.4 31.4 %all-to-all-start.3 = ((bf16[128,30,128]{2,1,0:T(8,128)(2,1)}), bf16[128,30,128]{2,1,0:T(8,128)(2,1)}, u32[]{:S(2)}, u32[]{:S(2)}) async-start(bf16[128,30,128]{2,1,0:T(8,128)(2,1)} %convert_element_type.198), calls=%async_computation.3 | async-start | bytes 2097152 | tf_op jit(solution)/shard_map/all_to_all | solution.py:111
  378.8 3.0 copy-start.15
  378.8 3.0 copy-start.34
  387.8 3.1 copy-start.7
  387.8 4.2 copy-start.6
  394.9 33.5 %all-to-all-start.1 = ((bf16[128,30,128]{2,1,0:T(8,128)(2,1)}), bf16[128,30,128]{2,1,0:T(8,128)(2,1)S(1)}, u32[]{:S(2)}, u32[]{:S(2)}) async-start(bf16[128,30,128]{2,1,0:T(8,128)(2,1)} %copy.138), calls=%async_computation.1 | async-start | bytes 2097152 | tf_op jit(solution)/shard_map/all_to_all | solution.py:111
  404.6 231.3 %all-reduce.9.cloned.1.call-start = ((), (), s32[]{:S(2)}) async-start(), calls=%async_computation.5 | async-start | bytes 2752512 | tf_op jit(solution)/shard_map/psum | solution.py:182
  415.5 2.7 copy-start.4
  415.5 2.7 copy-start.22
  427.0 214.3 %all-gather.2.cloned.1.call-start = ((), (), s32[]{:S(2)}) async-start(), calls=%async_computation.4 | async-start | bytes 16711680 | tf_op jit(solution)/shard_map/all_gather | solution.py:8
  641.4 8.7 %copy-start.16 = (f32[3840,128]{1,0:T(8,128)S(1)}, f32[3840,128]{1,0:T(8,128)}, u32[]{:S(2)}) copy-start(f32[3840,128]{1,0:T(8,128)} %fusion.50) | copy-start | bytes 5898244
  (22 other events, 35.8 us)
Sparse Core Ops, SparseCore 0:
  427.2 208.6 all-reduce.8
Sparse Core Ops, SparseCore 1:
  431.9 106.7 all-gather.1
